TPU v7x, 512 devices: a whole 4x8x8 slice. The times are simulated.
512 devices in a mesh: layer: 8 (over z), row: 64 (over y, x, core).
Axes of the slice: x: 4, y: 8, z: 8, core: 2. Of those that a mesh axis runs over, the one named last changes fastest.
Arguments:
- left_factors: bfloat16 [8, 65536, 128], P('layer', 'row'), may hold values from -0.1875 to 0.1875
- right_factors: bfloat16 [8, 65536, 128], P('layer', 'row'), may hold values from -0.1875 to 0.1875
- sketch: bfloat16 [65536, 128], P('row'), may hold values from -0.1875 to 0.1875
- row_basis: bfloat16 [65536, 128], P('row'), may hold values from -0.4375 to 0.4375
- inverse_diag: bfloat16 [65536, 1024], P('row'), may hold values from -0.0625 to 1.44125, as said below
- right_side: bfloat16 [65536, 4096], P('row', 'layer'), may hold values from -6 to 6
- incoming: float32 [128, 4096], P(None, 'layer'), may hold values from -6 to 6
Outputs:
- solution: bfloat16 [65536, 4096], P('row', 'layer')
Inputs may be any that keep to these rules, and one draw needn't show every extreme that they name: `inverse_diag`: each block of 1024 rows is the inverse of that row group's diagonal tile.
All inputs are finite; a program needn't handle non-finite values.
Results may differ from a plain program's by a relative error of at most 0.0095.
Values may be sent and summed in bfloat16 or wider, within the bound.
A program may use at most 128 MiB of HBM per device.

v0:
```python
import jax
import jax.numpy as jnp
from jax import lax
from jax.sharding import PartitionSpec as P


def shifted(value, axis, steps):
    count = lax.axis_size(axis)
    leading, last = (max(0, -steps), min(count, count - steps))
    return lax.ppermute(value, axis, [(source, source + steps) for source in range(leading, last)])


def entering(value, axis, combine, identity):
    count, here = (lax.axis_size(axis), lax.axis_index(axis))
    everything = jax.tree.map(lambda part: lax.all_gather(part, axis), value)
    start = jax.tree.map(
        lambda part, zero: jnp.broadcast_to(jnp.asarray(zero, part.dtype), part.shape),
        value,
        identity,
    )

    def lap(k, before):
        reached = k < here
        new = combine(before, jax.tree.map(lambda part: part[k], everything))
        return jax.tree.map(lambda a, b: jnp.where(reached, a, b), new, before)

    return lax.fori_loop(0, count, lap, start)


def project(basis, vectors):
    return lax.dot_general(
        basis, vectors, (((0,), (0,)), ((), ())), preferred_element_type=jnp.float32
    )


def body(left_factors, right_factors, sketch, row_basis, inverse_diag, right_side, incoming):
    full = lax.Precision.HIGHEST
    rank = sketch.shape[1]
    width = right_side.shape[1]
    core = project(right_factors[0], sketch).astype(jnp.bfloat16)
    partial_range = -jnp.dot(left_factors[0], core, preferred_element_type=jnp.float32)
    tile_range = lax.psum(partial_range, "layer").astype(jnp.bfloat16)
    applied = jnp.dot(inverse_diag, right_side, preferred_element_type=jnp.float32).astype(
        jnp.bfloat16
    )
    gain = jnp.dot(inverse_diag, tile_range, preferred_element_type=jnp.float32).astype(
        jnp.bfloat16
    )

    def combine(earlier, later):
        return (
            jnp.dot(later[0], earlier[0], precision=full),
            jnp.dot(later[0], earlier[1], precision=full) + later[1],
        )

    identity = (jnp.eye(rank, dtype=jnp.float32), jnp.zeros((rank, width), jnp.float32))
    joined = jnp.concatenate([applied, gain], axis=1)
    carried = shifted(joined, "row", 1)
    step_map = -project(row_basis, carried[:, width:])
    step_shift = project(row_basis, carried[:, :width])
    first_group = lax.axis_index("row") == 0
    step_shift = jnp.where(first_group, incoming, step_shift)
    prefix = entering((step_map, step_shift), "row", combine, identity)
    coupled = jnp.dot(step_map, prefix[1], precision=full) + step_shift
    result = applied.astype(jnp.float32) - jnp.dot(
        gain.astype(jnp.float32), coupled, precision=full
    )
    return result.astype(jnp.bfloat16)


def solution(mesh):
    return jax.shard_map(
        body,
        mesh=mesh,
        in_specs=(
            P("layer", "row", None),
            P("layer", "row", None),
            P("row", None),
            P("row", None),
            P("row", None),
            P("row", "layer"),
            P(None, "layer"),
        ),
        out_specs=P("row", "layer"),
        check_vma=False,
    )
```

profile of v0, /device:TPU:56, one launch (start us, length us, event | category | flops | bytes accessed | tf_op | source)
XLA Modules:
  0.0 387.8 jit_solution(16829505180996091301)
XLA Ops:
  6.5 1.8 fusion.8
  8.3 42.5 %all-reduce.1 = bf16[1024,128]{0,1:T(8,128)(2,1)S(1)} all-reduce(f32[1024,128]{0,1:T(8,128)S(1)} %fusion.8), channel_id=1, replica_groups=mesh['layer'=8,'row'=64] {'layer'}, use_global_device_ids=true, to_apply=%region_0.0 | all-reduce | flops 131072 | bytes 786432 | tf_op jit(solution)/shard_map/psum | solution.py:42
  53.5 2.1 collective-permute-start
  55.5 19.1 %collective-permute-done = bf16[1024,640]{0,1:T(8,128)(2,1)S(1)} collective-permute-done((bf16[1024,640]{0,1:T(8,128)(2,1)S(1)}, bf16[1024,640]{0,1:T(8,128)(2,1)S(1)}, u32[]{:S(2)}, u32[]{:S(2)}) %collective-permute-start) | collective-permute-done | bytes 1310752 | tf_op jit(solution)/shard_map/ppermute | solution.py:10
  76.7 2.4 fusion.9
  79.1 73.2 %all-gather.5.cloned.1.call-done = f32[8192,128]{0,1:T(8,128)} async-done(((f32[128,128]{0,1:T(8,128)}), f32[8192,128]{0,1:T(8,128)}) %all-gather.5.cloned.1.call-update) | async-done | bytes 4194320 | tf_op jit(solution)/shard_map/all_gather | solution.py:15
  152.3 5.6 %copy.14 = f32[8192,128]{1,0:T(8,128)} copy(f32[8192,128]{0,1:T(8,128)} %all-gather.5.cloned.1.call-done) | data formatting | bytes 8388608
  158.0 107.6 %all-gather.7.cloned.1.call-done = f32[8192,512]{0,1:T(8,128)} async-done(((f32[128,512]{0,1:T(8,128)}), f32[8192,512]{0,1:T(8,128)}) %all-gather.7.cloned.1.call-update) | async-done | bytes 16777232 | tf_op jit(solution)/shard_map/all_gather | solution.py:15
  265.6 17.4 %copy.15 = f32[8192,512]{1,0:T(8,128)} copy(f32[8192,512]{0,1:T(8,128)} %all-gather.7.cloned.1.call-done) | data formatting | bytes 33554432
  283.0 91.2 %while.14 = (s32[]{:T(128)}, f32[128,512]{1,0:T(8,128)S(1)}, s32[]{:T(128)}, f32[64,128,128]{2,1,0:T(8,128)}, f32[64,128,512]{2,1,0:T(8,128)}, /*index=5*/s32[]{:T(128)}, s32[]{:T(128)}) while((s32[]{:T(128)}, f32[128,512]{1,0:T(8,128)S(1)}, s32[]{:T(128)}, f32[64,128,128]{2,1,0:T(8,128)}, f32[64,128,512]{2,1,0:T(8,128)}, ...), condition=%wide.region_2.3_spmd.clone, body=%wide.region_1.2_spmd.clone.sunk | while | flops 100925440 | bytes 1641055 | solution.py:27
  283.0 1.4 fusion.32
  284.5 1.4 fusion.32
  285.9 1.4 fusion.32
  287.3 1.4 fusion.32
  288.7 1.4 fusion.32
  290.2 1.4 fusion.32
  291.6 1.4 fusion.32
  293.0 1.4 fusion.32
  294.4 1.4 fusion.32
  295.9 1.4 fusion.32
  297.3 1.4 fusion.32
  298.7 1.4 fusion.32
  300.1 1.4 fusion.32
  301.6 1.4 fusion.32
  303.0 1.4 fusion.32
  304.4 1.4 fusion.32
  305.8 1.4 fusion.32
  307.3 1.4 fusion.32
  308.7 1.4 fusion.32
  310.1 1.4 fusion.32
  311.5 1.4 fusion.32
  313.0 1.4 fusion.32
  314.4 1.4 fusion.32
  315.8 1.4 fusion.32
  317.2 1.4 fusion.32
  318.7 1.4 fusion.32
  320.1 1.4 fusion.32
  321.5 1.4 fusion.32
  322.9 1.4 fusion.32
  324.4 1.4 fusion.32
  325.8 1.4 fusion.32
  327.2 1.4 fusion.32
  328.6 1.4 fusion.32
  332.9 1.4 fusion.32
  334.3 1.4 fusion.32
  335.8 1.4 fusion.32
  338.6 1.4 fusion.32
  341.5 1.4 fusion.32
  342.9 1.4 fusion.32
  347.2 1.4 fusion.32
  348.6 1.4 fusion.32
  350.0 1.4 fusion.32
  352.9 1.4 fusion.32
  355.7 1.4 fusion.32
  357.1 1.4 fusion.32
  361.4 1.4 fusion.32
  362.8 1.4 fusion.32
  364.3 1.4 fusion.32
  367.1 1.4 fusion.32
  370.0 1.4 fusion.32
  371.4 1.4 fusion.32
  374.2 1.5 convolution_add_fusion.1
  375.7 2.9 subtract_convert_fusion
  378.7 2.3 copy.12
  (101 shorter events, 23.7 us)
Async XLA Ops:
  6.5 44.2 %copy-start = (bf16[1024,1024]{1,0:T(8,128)(2,1)S(1)}, bf16[1024,1024]{1,0:T(8,128)(2,1)}, u32[]{:S(2)}) copy-start(bf16[1024,1024]{1,0:T(8,128)(2,1)} %param.13) | copy-start | bytes 6291460
  6.5 145.8 %all-gather.5.cloned.1.call-start = ((), (), s32[]{:S(2)}) async-start(), calls=%async_computation | async-start | bytes 4259840 | tf_op jit(solution)/shard_map/all_gather | solution.py:15
  50.8 1.2 copy-start.6
  52.0 1.3 copy-start.1
  53.3 21.3 %copy-start.4 = (bf16[1024,128]{1,0:T(8,128)(2,1)S(1)}, bf16[1024,128]{1,0:T(8,128)(2,1)}, u32[]{:S(2)}) copy-start(bf16[1024,128]{1,0:T(8,128)(2,1)} %param.12) | copy-start | bytes 786436
  53.3 22.5 %copy-start.3 = (f32[128,512]{1,0:T(8,128)S(1)}, f32[128,512]{1,0:T(8,128)}, u32[]{:S(2)}) copy-start(f32[128,512]{1,0:T(8,128)} %param.15) | copy-start | bytes 786436
  53.5 21.2 %collective-permute-start = (bf16[1024,640]{0,1:T(8,128)(2,1)S(1)}, bf16[1024,640]{0,1:T(8,128)(2,1)S(1)}, u32[]{:S(2)}, u32[]{:S(2)}) collective-permute-start(bf16[1024,640]{0,1:T(8,128)(2,1)S(1)} %pad_maximum_fusion), channel_id=1, source_target_pairs={{0,1},{1,2},{2,3},{3,4},{4,5},{5,6},{6,7},{7,8},{8,9},{9,10},{10,1... | collective-permute-start | bytes 3932168 | tf_op jit(solution)/shard_map/ppermute | solution.py:10
  74.6 1.1 copy-start.5
  75.8 189.8 %all-gather.7.cloned.1.call-start = ((), (), s32[]{:S(2)}) async-start(), calls=%async_computation.1 | async-start | bytes 17039360 | tf_op jit(solution)/shard_map/all_gather | solution.py:15
  283.0 91.2 %copy-start.2 = (f32[128,128]{1,0:T(8,128)S(1)}, f32[128,128]{1,0:T(8,128)}, u32[]{:S(2)}) copy-start(f32[128,128]{1,0:T(8,128)} %convolution_negate_fusion.1) | copy-start | bytes 196612
Sparse Core Ops, SparseCore 0:
  75.9 76.3 all-gather.4
  155.6 109.9 all-gather.6
where the time goes:
time: 392 us; the launch traced here: 388 us
  waiting for transfers between devices  200 us (51%)
  matrix products  99.4 us (25%)
  blocking collectives  42.5 us (11%)
  local copies, waits for them, and re-layouts  27.9 us (7%)
  between operations  13.5 us (3%)
    all_gather x2, waiting for transfers between devices, entering(): everything = jax.tree.map(lambda part: lax.all_gather(part, axis), value)  181 us
    dot_general x64, matrix products, combine(): jnp.dot(later[0], earlier[1], precision=full) + later[1]  87.6 us
    psum x1, blocking collectives, body(): tile_range = lax.psum(partial_range, 'layer').astype(jnp.bfloat16)  42.5 us
    unnamed x17, local copies, waits for them, and re-layouts  24.4 us
    ppermute x1, waiting for transfers between devices, shifted(): lax.ppermute(value, axis, [(source, source + steps) for source in range(l...  19.1 us
  transfers between devices with their start and end apart: 3, of which 3 were waited for; matrix products, arithmetic and copies ran while one was open for 2% of the time, Pallas kernels for 0%

commit v1 on v0

v1 whole, which is shorter than its diff:
```python
import functools

import jax
import jax.numpy as jnp
from jax import lax
from jax.experimental import pallas as pl
from jax.experimental.pallas import tpu as pltpu
from jax.sharding import PartitionSpec as P

MESH = pl.DeviceIdType.MESH
INNER = 8
BF16 = jnp.bfloat16
F32 = jnp.float32


def mm(a, b, ca=1, cb=0):
    return lax.dot_general(a, b, (((ca,), (cb,)), ((), ())), preferred_element_type=F32)


def split(value):
    high = value.astype(BF16)
    return high, (value - high.astype(F32)).astype(BF16)


def far_first(n):
    return sorted(range(1, n), key=lambda o: -min(o, n - o))


RS, SH, MZ, GZ, MI, OU, CB, BS = range(8)


def kernel(
    nz, ni, ny,
    left, right, sketch, basis, inverse, rhs, incoming,
    out,
    v_left, v_right, v_sketch, v_basis, v_inv, v_invt, v_rhs, v_inc, v_app,
    part, part_in, shift, shift_in, maps, gain_t, gain, pre_s, pre_m, total, total_in,
    inc_t, carry, coup, coup_in,
    load_sem, send_sem, recv_sem,
):
    z, row = lax.axis_index("layer"), lax.axis_index("row")
    y, i = row // ni, row % ni
    rows = row - i
    n_row = ni * ny
    order, rank = v_inv.shape[0], v_sketch.shape[1]
    width = v_rhs.shape[1]
    cols = width // ni
    thick = rank // nz

    loads = [
        pltpu.make_async_copy(source, target, load_sem.at[k])
        for k, (source, target) in enumerate(
            [(right, v_right), (sketch, v_sketch), (left, v_left), (inverse, v_inv), (rhs, v_rhs), (incoming, v_inc)]
        )
    ]
    for load in loads:
        load.start()

    barrier = pltpu.get_barrier_semaphore()

    def greet(layer, target):
        pl.semaphore_signal(barrier, inc=1, device_id=(layer, target), device_id_type=MESH)

    for o in range(1, nz):
        greet((z + o) % nz, row)
    for o in range(1, ni):
        greet(z, rows + (i + o) % ni)
    for o in range(1, ny):
        greet(z, ((y + o) % ny) * ni + i)
    greet(z, (row + 1) % n_row)
    greet(z, (row + n_row - 1) % n_row)

    def send(kind, slot, source, target, layer, dest):
        copy = pltpu.make_async_remote_copy(
            src_ref=source,
            dst_ref=target,
            send_sem=send_sem.at[kind, slot],
            recv_sem=recv_sem.at[kind, slot],
            device_id=(layer, dest),
            device_id_type=MESH,
        )
        copy.start()
        return copy

    def await_slot(kind, slot, target):
        pltpu.make_async_remote_copy(
            src_ref=target,
            dst_ref=target,
            send_sem=send_sem.at[kind, slot],
            recv_sem=recv_sem.at[kind, slot],
            device_id=(z, row),
            device_id_type=MESH,
        ).wait_recv()

    sent = []

    loads[0].wait()
    loads[1].wait()
    core_t = mm(v_sketch[...], v_right[...], 0, 0).astype(BF16)
    loads[2].wait()
    part[...] = mm(core_t, v_left[...], 1, 1).reshape(part.shape)

    pl.semaphore_wait(barrier, (nz - 1) + (ni - 1) + (ny - 1) + 2)
    for o in far_first(nz):
        peer = (z + o) % nz
        sent.append(send(RS, o, part.at[peer], part_in.at[z], peer, row))
    sent.append(send(BS, 0, basis, v_basis, z, (row + n_row - 1) % n_row))

    for load in loads[3:]:
        load.wait()
    step = 256

    def apply_inverse(t, carried):
        at = pl.ds(pl.multiple_of(t * step, step), step)
        v_app[at, :] = mm(v_inv[at, :], v_rhs[...]).astype(BF16)
        return carried

    lax.fori_loop(0, order // step, apply_inverse, 0)
    await_slot(BS, 0, v_basis)
    step_shift = mm(v_basis[...], v_app[...], 0, 0)
    shift[...] = step_shift.T.reshape(shift.shape)
    for o in range(1, ni):
        peer = (i + o) % ni
        sent.append(send(SH, o, shift.at[peer], shift_in.at[i], z, rows + peer))
    shift_in[i] = shift[i]
    inc_t[...] = v_inc[...].T.reshape(inc_t.shape)

    for t in range(order // step):
        v_invt[:, t * step : (t + 1) * step] = v_inv[t * step : (t + 1) * step, :].T

    summed = part[z]
    for o in far_first(nz)[::-1]:
        source = (z + nz - o) % nz
        await_slot(RS, o, part_in.at[source])
        summed = summed + part_in[source]
    range_t = (-summed).astype(BF16)
    gain_part = mm(range_t, v_invt[...]).astype(BF16)
    gain_t[z] = gain_part
    high, low = split(-mm(gain_part, v_basis[...]))
    maps[i, z] = jnp.concatenate([high, low], axis=1)
    for o in far_first(nz):
        sent.append(send(MZ, o, maps.at[i, z], maps.at[i, z], (z + o) % nz, row))
    for o in far_first(nz):
        sent.append(send(GZ, o, gain_t.at[z], gain_t.at[z], (z + o) % nz, row))
    for o in far_first(nz)[::-1]:
        await_slot(MZ, o, maps.at[i, (z + nz - o) % nz])
    for o in range(1, ni):
        sent.append(send(MI, o, maps.at[i], maps.at[i], z, rows + (i + o) % ni))

    for o in range(1, ni):
        await_slot(SH, o, shift_in.at[(i + ni - o) % ni])

    def arrive(k):
        @pl.when(k != i)
        def _():
            await_slot(MI, (i + ni - k) % ni, maps.at[k])

    arrive(0)
    first = maps[0].reshape(rank, 2 * rank).astype(F32)
    state = jnp.concatenate([shift_in[0], first[:, :rank] + first[:, rank:]], axis=0)
    tall = cols + rank
    for k in range(1, ni):
        pre_s[k] = state[:cols]
        pre_m[:, k * rank : (k + 1) * rank] = state[cols:].astype(BF16)
        arrive(k)
        product = mm(jnp.concatenate(split(state), axis=0), maps[k].reshape(rank, 2 * rank))
        state = product[:tall, :rank] + (product[:tall, rank:] + product[tall:, :rank])
        state = jnp.concatenate([state[:cols] + shift_in[k], state[cols:]], axis=0)
    total[...] = state.astype(BF16)

    for d in range(ny - 1, 0, -1):

        @pl.when(y + d < ny)
        def _():
            send(OU, d, total, total_in.at[y], z, row + d * ni)

    for o in far_first(nz)[::-1]:
        await_slot(GZ, o, gain_t.at[(z + nz - o) % nz])
    gain[...] = gain_t[...].reshape(rank, order).T

    carry[...] = inc_t[i]
    for k in range(ny - 1):

        @pl.when(k < y)
        def _():
            await_slot(OU, y - k, total_in.at[k])
            product = mm(jnp.concatenate(split(carry[...]), axis=0), total_in[k, cols:, :])
            carry[...] = product[:cols] + product[cols:] + total_in[k, :cols, :].astype(F32)

    start = carry[...]
    coup[0] = start.astype(BF16)
    product = mm(jnp.concatenate(split(start), axis=0), pre_m[:, rank:])
    product = product[:cols] + product[cols:]
    for k in range(1, ni):
        coup[k] = (product[:, (k - 1) * rank : k * rank] + pre_s[k]).astype(BF16)
    for o in range(1, ni):
        peer = (i + o) % ni
        sent.append(send(CB, o, coup.at[peer], coup_in.at[i], z, rows + peer))
    coup_in[i] = coup[i]
    for o in range(1, ni):
        await_slot(CB, o, coup_in.at[(i + ni - o) % ni])

    coupled_t = coup_in[...].reshape(width, rank)
    for t in range(order // step):
        at = slice(t * step, (t + 1) * step)
        out[at, :] = (v_app[at, :].astype(F32) - mm(gain[at, :], coupled_t, 1, 1)).astype(BF16)

    for copy in sent:
        copy.wait_send()
    for d in range(1, ny):

        @pl.when(y + d < ny)
        def _():
            pltpu.make_async_remote_copy(
                src_ref=total,
                dst_ref=total_in.at[y],
                send_sem=send_sem.at[OU, d],
                recv_sem=recv_sem.at[OU, d],
                device_id=(z, row + d * ni),
                device_id_type=MESH,
            ).wait_send()


def solution(mesh, inner=INNER):
    nz, n_row = mesh.shape["layer"], mesh.shape["row"]
    ni, ny = inner, n_row // inner

    def body(left, right, sketch, row_basis, inverse, rhs, incoming):
        order, rank = sketch.shape
        width = rhs.shape[1]
        cols, thick = width // ni, rank // nz
        vm = pltpu.VMEM
        return pl.pallas_call(
            functools.partial(kernel, nz, ni, ny),
            out_shape=jax.ShapeDtypeStruct((order, width), BF16),
            in_specs=[pl.BlockSpec(memory_space=pltpu.HBM)] * 7,
            out_specs=pl.BlockSpec(memory_space=pltpu.VMEM),
            scratch_shapes=[
                vm((order, rank), BF16),
                vm((order, rank), BF16),
                vm((order, rank), BF16),
                vm((order, rank), BF16),
                vm((order, order), BF16),
                vm((order, order), BF16),
                vm((order, width), BF16),
                vm((rank, width), F32),
                vm((order, width), BF16),
                vm((nz, thick, order), F32),
                vm((nz, thick, order), F32),
                vm((ni, cols, rank), F32),
                vm((ni, cols, rank), F32),
                vm((ni, nz, thick, 2 * rank), BF16),
                vm((nz, thick, order), BF16),
                vm((order, rank), BF16),
                vm((ni, cols, rank), F32),
                vm((rank, ni * rank), BF16),
                vm((cols + rank, rank), BF16),
                vm((ny, cols + rank, rank), BF16),
                vm((ni, cols, rank), F32),
                vm((cols, rank), F32),
                vm((ni, cols, rank), BF16),
                vm((ni, cols, rank), BF16),
                pltpu.SemaphoreType.DMA((6,)),
                pltpu.SemaphoreType.DMA((8, 8)),
                pltpu.SemaphoreType.DMA((8, 8)),
            ],
            compiler_params=pltpu.CompilerParams(
                collective_id=0, has_side_effects=True, vmem_limit_bytes=48 << 20
            ),
        )(*[pltpu.with_memory_space_constraint(a, pltpu.HBM) for a in (left[0], right[0], sketch, row_basis, inverse, rhs, incoming)])

    return jax.shard_map(
        body,
        mesh=mesh,
        in_specs=(
            P("layer", "row", None),
            P("layer", "row", None),
            P("row", None),
            P("row", None),
            P("row", None),
            P("row", "layer"),
            P(None, "layer"),
        ),
        out_specs=P("row", "layer"),
        check_vma=False,
    )
```

time: 392 us -> 56.6 us (0.14)
  the two profiles are of different devices: /device:TPU:56 before, /device:TPU:41 now
where the time goes in v1:
time: 56.6 us; the launch traced here: 56.4 us
  Pallas kernels  55.5 us (98%)
  local copies, waits for them, and re-layouts  0.97 us (2%)
    pallas_call x1, Pallas kernels, body(): pl.pallas_call(functools.partial(kernel, nz, ni, ny), out_shape=jax.Shape...  55.5 us

profile of v1, /device:TPU:41, one launch (start us, length us, event | category | flops | bytes accessed | tf_op | source)
XLA Modules:
  0.0 56.4 jit_solution(14580600023736534041)
XLA Ops:
  0.0 55.5 %shard_map.73 = bf16[1024,512]{1,0:T(8,128)(2,1)S(1)} custom-call(bf16[1024,128]{1,0:T(8,128)(2,1)} %bitcast.2, bf16[1024,128]{1,0:T(8,128)(2,1)} %bitcast.3, bf16[1024,128]{1,0:T(8,128)(2,1)} %sketch.1, bf16[1024,128]{1,0:T(8,128)(2,1)} %basis.1, bf16[1024,1024]{1,0:T(8,128)(2,1)} %inverse.1, bf16[1024,512]{1,0:T(8,128)(2,1)} %rhs.1, f32[128,512]{1,0:T(8,128)} %incoming.1), custom_call_target="tpu_custom_call" | custom-call | tf_op jit(solution)/shard_map/pallas_call | solution.py:233
  55.5 1.0 %copy.9 = bf16[1024,512]{1,0:T(8,128)(2,1)} copy(bf16[1024,512]{1,0:T(8,128)(2,1)S(1)} %shard_map.73) | data formatting | bytes 2097152

commit v2 on v1

--- a/solution.py
+++ b/solution.py
@@ -9,6 +9,7 @@
 
 MESH = pl.DeviceIdType.MESH
 INNER = 8
+CUTS = 1
 BF16 = jnp.bfloat16
 F32 = jnp.float32
 
@@ -26,7 +27,7 @@
     return sorted(range(1, n), key=lambda o: -min(o, n - o))
 
 
-RS, SH, MZ, GZ, MI, OU, CB, BS = range(8)
+SH, MZ, GZ, MI, OU, CB, BS = range(7)
 
 
 def kernel(
@@ -34,9 +35,9 @@
     left, right, sketch, basis, inverse, rhs, incoming,
     out,
     v_left, v_right, v_sketch, v_basis, v_inv, v_invt, v_rhs, v_inc, v_app,
-    part, part_in, shift, shift_in, maps, gain_t, gain, pre_s, pre_m, total, total_in,
+    part, ring_in, ring_out, shift, shift_in, maps, gain_t, gain, pre_s, pre_m, total, total_in,
     inc_t, carry, coup, coup_in,
-    load_sem, send_sem, recv_sem,
+    load_sem, send_sem, recv_sem, ring_send, ring_recv,
 ):
     z, row = lax.axis_index("layer"), lax.axis_index("row")
     y, i = row // ni, row % ni
@@ -101,9 +102,48 @@
     part[...] = mm(core_t, v_left[...], 1, 1).reshape(part.shape)
 
     pl.semaphore_wait(barrier, (nz - 1) + (ni - 1) + (ny - 1) + 2)
-    for o in far_first(nz):
-        peer = (z + o) % nz
-        sent.append(send(RS, o, part.at[peer], part_in.at[z], peer, row))
+    piece = order // CUTS
+
+    def ring_views(way, far, half, cut):
+        rows_at, cols_at = pl.ds(half * (thick // 2), thick // 2), pl.ds(cut * piece, piece)
+        owner = (z + far) % nz if way == 0 else (z + nz - far) % nz
+        return (
+            part.at[owner, rows_at, cols_at],
+            ring_out.at[way, far - 1, rows_at, cols_at],
+            ring_in.at[way, far - 1, rows_at, cols_at],
+        )
+
+    def ring_copy(way, far, half, cut, source):
+        return pltpu.make_async_remote_copy(
+            src_ref=source,
+            dst_ref=ring_views(way, far, half, cut)[2],
+            send_sem=ring_send.at[way, far - 1, half * CUTS + cut],
+            recv_sem=ring_recv.at[way, far - 1, half * CUTS + cut],
+            device_id=((z + 1) % nz if way == 0 else (z + nz - 1) % nz, row),
+            device_id_type=MESH,
+        )
+
+    longest, shortest = nz // 2, (nz - 1) // 2
+    chains = [(way, half, longest if way == half else shortest) for way, half in ((0, 0), (1, 1), (0, 1), (1, 0))]
+
+    def ring_round(turn):
+        for way, half, most in chains:
+            far = most - turn
+            if far < 1:
+                continue
+            for cut in range(CUTS):
+                own, staged, _ = ring_views(way, far, half, cut)
+                if turn == 0:
+                    source = own
+                else:
+                    ring_copy(way, far + 1, half, cut, own).wait_recv()
+                    staged[...] = ring_views(way, far + 1, half, cut)[2][...] + own[...]
+                    source = staged
+                copy = ring_copy(way, far, half, cut, source)
+                copy.start()
+                sent.append(copy)
+
+    ring_round(0)
     sent.append(send(BS, 0, basis, v_basis, z, (row + n_row - 1) % n_row))
 
     for load in loads[3:]:
@@ -116,6 +156,11 @@
         return carried
 
     lax.fori_loop(0, order // step, apply_inverse, 0)
+    ring_round(1)
+    for t in range(order // step):
+        v_invt[:, t * step : (t + 1) * step] = v_inv[t * step : (t + 1) * step, :].T
+    inc_t[...] = v_inc[...].T.reshape(inc_t.shape)
+    ring_round(2)
     await_slot(BS, 0, v_basis)
     step_shift = mm(v_basis[...], v_app[...], 0, 0)
     shift[...] = step_shift.T.reshape(shift.shape)
@@ -123,16 +168,22 @@
         peer = (i + o) % ni
         sent.append(send(SH, o, shift.at[peer], shift_in.at[i], z, rows + peer))
     shift_in[i] = shift[i]
-    inc_t[...] = v_inc[...].T.reshape(inc_t.shape)
-
-    for t in range(order // step):
-        v_invt[:, t * step : (t + 1) * step] = v_inv[t * step : (t + 1) * step, :].T
-
+    for turn in range(3, longest):
+        ring_round(turn)
+    for way, half, most in chains[::-1]:
+        if most > 0:
+            for cut in range(CUTS):
+                own, _, arrived = ring_views(way, 1, half, cut)
+                ring_copy(way, 1, half, cut, own).wait_recv()
     summed = part[z]
-    for o in far_first(nz)[::-1]:
-        source = (z + nz - o) % nz
-        await_slot(RS, o, part_in.at[source])
-        summed = summed + part_in[source]
+    for way in range(2):
+        halves = [
+            ring_in[way, 0, half * (thick // 2) : (half + 1) * (thick // 2), :]
+            if (longest if way == half else shortest) > 0
+            else jnp.zeros((thick // 2, order), F32)
+            for half in range(2)
+        ]
+        summed = summed + jnp.concatenate(halves, axis=0)
     range_t = (-summed).astype(BF16)
     gain_part = mm(range_t, v_invt[...]).astype(BF16)
     gain_t[z] = gain_part
@@ -140,12 +191,12 @@
     maps[i, z] = jnp.concatenate([high, low], axis=1)
     for o in far_first(nz):
         sent.append(send(MZ, o, maps.at[i, z], maps.at[i, z], (z + o) % nz, row))
+    for o in far_first(nz)[::-1]:
+        await_slot(MZ, o, maps.at[i, (z + nz - o) % nz])
+    for o in range(1, ni):
+        sent.append(send(MI, o, maps.at[i], maps.at[i], z, rows + (i + o) % ni))
     for o in far_first(nz):
         sent.append(send(GZ, o, gain_t.at[z], gain_t.at[z], (z + o) % nz, row))
-    for o in far_first(nz)[::-1]:
-        await_slot(MZ, o, maps.at[i, (z + nz - o) % nz])
-    for o in range(1, ni):
-        sent.append(send(MI, o, maps.at[i], maps.at[i], z, rows + (i + o) % ni))
 
     for o in range(1, ni):
         await_slot(SH, o, shift_in.at[(i + ni - o) % ni])
@@ -167,25 +218,45 @@
         state = product[:tall, :rank] + (product[:tall, rank:] + product[tall:, :rank])
         state = jnp.concatenate([state[:cols] + shift_in[k], state[cols:]], axis=0)
     total[...] = state.astype(BF16)
-
-    for d in range(ny - 1, 0, -1):
-
-        @pl.when(y + d < ny)
+    carry[...] = inc_t[i]
+
+    def follow(block, added):
+        product = mm(jnp.concatenate(split(carry[...]), axis=0), block)
+        return product[:cols] + product[cols:] + added
+
+    def outer_copies(act):
+        @pl.when(y == 0)
         def _():
-            send(OU, d, total, total_in.at[y], z, row + d * ni)
+            for d in range(ny - 1, 0, -1):
+                act(d, total.at[pl.ds(0, cols)], total_in.at[0, pl.ds(0, cols)])
+
+        for d in range(ny - 2, 0, -1):
+
+            @pl.when(jnp.logical_and(y > 0, y + d < ny))
+            def _():
+                act(d, total, total_in.at[y])
+
+    @pl.when(y == 0)
+    def _():
+        total[:cols, :] = follow(total[cols:, :], state[:cols]).astype(BF16)
+
+    outer_copies(lambda d, source, target: send(OU, d, source, target, z, row + d * ni))
 
     for o in far_first(nz)[::-1]:
         await_slot(GZ, o, gain_t.at[(z + nz - o) % nz])
     gain[...] = gain_t[...].reshape(rank, order).T
 
-    carry[...] = inc_t[i]
-    for k in range(ny - 1):
+    @pl.when(y > 0)
+    def _():
+        await_slot(OU, y, total_in.at[0, pl.ds(0, cols)])
+        carry[...] = total_in[0, :cols, :].astype(F32)
+
+    for k in range(1, ny - 1):
 
         @pl.when(k < y)
         def _():
             await_slot(OU, y - k, total_in.at[k])
-            product = mm(jnp.concatenate(split(carry[...]), axis=0), total_in[k, cols:, :])
-            carry[...] = product[:cols] + product[cols:] + total_in[k, :cols, :].astype(F32)
+            carry[...] = follow(total_in[k, cols:, :], total_in[k, :cols, :].astype(F32))
 
     start = carry[...]
     coup[0] = start.astype(BF16)
@@ -207,18 +278,17 @@
 
     for copy in sent:
         copy.wait_send()
-    for d in range(1, ny):
-
-        @pl.when(y + d < ny)
-        def _():
-            pltpu.make_async_remote_copy(
-                src_ref=total,
-                dst_ref=total_in.at[y],
-                send_sem=send_sem.at[OU, d],
-                recv_sem=recv_sem.at[OU, d],
-                device_id=(z, row + d * ni),
-                device_id_type=MESH,
-            ).wait_send()
+    def outer_sent(d, source, target):
+        pltpu.make_async_remote_copy(
+            src_ref=source,
+            dst_ref=target,
+            send_sem=send_sem.at[OU, d],
+            recv_sem=recv_sem.at[OU, d],
+            device_id=(z, row + d * ni),
+            device_id_type=MESH,
+        ).wait_send()
+
+    outer_copies(outer_sent)
 
 
 def solution(mesh, inner=INNER):
@@ -246,7 +316,8 @@
                 vm((rank, width), F32),
                 vm((order, width), BF16),
                 vm((nz, thick, order), F32),
-                vm((nz, thick, order), F32),
+                vm((2, max(nz // 2, 1), thick, order), F32),
+                vm((2, max(nz // 2, 1), thick, order), F32),
                 vm((ni, cols, rank), F32),
                 vm((ni, cols, rank), F32),
                 vm((ni, nz, thick, 2 * rank), BF16),
@@ -263,6 +334,8 @@
                 pltpu.SemaphoreType.DMA((6,)),
                 pltpu.SemaphoreType.DMA((8, 8)),
                 pltpu.SemaphoreType.DMA((8, 8)),
+                pltpu.SemaphoreType.DMA((2, 4, 2 * CUTS)),
+                pltpu.SemaphoreType.DMA((2, 4, 2 * CUTS)),
             ],
             compiler_params=pltpu.CompilerParams(
                 collective_id=0, has_side_effects=True, vmem_limit_bytes=48 << 20

time: 56.6 us -> 56.6 us (level)
  the two profiles are of different devices: /device:TPU:41 before, /device:TPU:56 now
where the time goes in v2:
time: 56.6 us; the launch traced here: 55.5 us
  Pallas kernels  54.5 us (96%)
  local copies, waits for them, and re-layouts  0.97 us (2%)
    pallas_call x1, Pallas kernels, body(): pl.pallas_call(functools.partial(kernel, nz, ni, ny), out_shape=jax.Shape...  54.5 us

profile of v2, /device:TPU:56, one launch (start us, length us, event | category | flops | bytes accessed | tf_op | source)
XLA Modules:
  0.0 55.5 jit_solution(1980215372094432817)
XLA Ops:
  0.0 54.5 %shard_map.73 = bf16[1024,512]{1,0:T(8,128)(2,1)S(1)} custom-call(bf16[1024,128]{1,0:T(8,128)(2,1)} %bitcast.2, bf16[1024,128]{1,0:T(8,128)(2,1)} %bitcast.3, bf16[1024,128]{1,0:T(8,128)(2,1)} %sketch.1, bf16[1024,128]{1,0:T(8,128)(2,1)} %basis.1, bf16[1024,1024]{1,0:T(8,128)(2,1)} %inverse.1, bf16[1024,512]{1,0:T(8,128)(2,1)} %rhs.1, f32[128,512]{1,0:T(8,128)} %incoming.1), custom_call_target="tpu_custom_call" | custom-call | tf_op jit(solution)/shard_map/pallas_call | solution.py:303
  54.5 1.0 %copy.9 = bf16[1024,512]{1,0:T(8,128)(2,1)} copy(bf16[1024,512]{1,0:T(8,128)(2,1)S(1)} %shard_map.73) | data formatting | bytes 2097152

commit v3 on v1

--- a/solution.py
+++ b/solution.py
@@ -26,7 +26,7 @@
     return sorted(range(1, n), key=lambda o: -min(o, n - o))
 
 
-RS, SH, MZ, GZ, MI, OU, CB, BS = range(8)
+RS, SH, MZ, GZ, MI, OU, CB, BS, FW, ME = range(10)
 
 
 def kernel(
@@ -36,7 +36,7 @@
     v_left, v_right, v_sketch, v_basis, v_inv, v_invt, v_rhs, v_inc, v_app,
     part, part_in, shift, shift_in, maps, gain_t, gain, pre_s, pre_m, total, total_in,
     inc_t, carry, coup, coup_in,
-    load_sem, send_sem, recv_sem,
+    block, merge_in, merged, load_sem, send_sem, recv_sem,
 ):
     z, row = lax.axis_index("layer"), lax.axis_index("row")
     y, i = row // ni, row % ni
@@ -101,9 +101,27 @@
     part[...] = mm(core_t, v_left[...], 1, 1).reshape(part.shape)
 
     pl.semaphore_wait(barrier, (nz - 1) + (ni - 1) + (ny - 1) + 2)
-    for o in far_first(nz):
+
+    merging = nz == 8
+    thin = thick // 2
+    low, high_rows = pl.ds(0, thin), pl.ds(thin, thin)
+
+    def give(o):
         peer = (z + o) % nz
-        sent.append(send(RS, o, part.at[peer], part_in.at[z], peer, row))
+        send(RS, o, part.at[peer], part_in.at[z], peer, row)
+
+    if merging:
+        across = (z + 4) % nz
+        sent.append(send(ME, 0, part.at[across, low], merge_in.at[0], (z + 1) % nz, row))
+        sent.append(send(ME, 1, part.at[across, high_rows], merge_in.at[1], (z + 7) % nz, row))
+        third, fifth = (z + 3) % nz, (z + 5) % nz
+        send(RS, 3, part.at[third, high_rows], part_in.at[z, high_rows], third, row)
+        send(RS, 5, part.at[fifth, low], part_in.at[z, low], fifth, row)
+        give(2)
+        give(6)
+    else:
+        for o in far_first(nz):
+            give(o)
     sent.append(send(BS, 0, basis, v_basis, z, (row + n_row - 1) % n_row))
 
     for load in loads[3:]:
@@ -116,6 +134,19 @@
         return carried
 
     lax.fori_loop(0, order // step, apply_inverse, 0)
+    for t in range(order // step):
+        v_invt[:, t * step : (t + 1) * step] = v_inv[t * step : (t + 1) * step, :].T
+    inc_t[...] = v_inc[...].T.reshape(inc_t.shape)
+    if merging:
+        await_slot(ME, 0, merge_in.at[0])
+        merged[0] = merge_in[0] + part[third, :thin, :]
+        send(RS, 3, merged.at[0], part_in.at[z, low], third, row)
+        await_slot(ME, 1, merge_in.at[1])
+        merged[1] = merge_in[1] + part[fifth, thin:, :]
+        send(RS, 5, merged.at[1], part_in.at[z, high_rows], fifth, row)
+        give(1)
+        give(7)
+
     await_slot(BS, 0, v_basis)
     step_shift = mm(v_basis[...], v_app[...], 0, 0)
     shift[...] = step_shift.T.reshape(shift.shape)
@@ -123,13 +154,10 @@
         peer = (i + o) % ni
         sent.append(send(SH, o, shift.at[peer], shift_in.at[i], z, rows + peer))
     shift_in[i] = shift[i]
-    inc_t[...] = v_inc[...].T.reshape(inc_t.shape)
-
-    for t in range(order // step):
-        v_invt[:, t * step : (t + 1) * step] = v_inv[t * step : (t + 1) * step, :].T
 
     summed = part[z]
-    for o in far_first(nz)[::-1]:
+    givers = [o for o in far_first(nz)[::-1] if not (merging and o == 4)]
+    for o in givers:
         source = (z + nz - o) % nz
         await_slot(RS, o, part_in.at[source])
         summed = summed + part_in[source]
@@ -140,12 +168,18 @@
     maps[i, z] = jnp.concatenate([high, low], axis=1)
     for o in far_first(nz):
         sent.append(send(MZ, o, maps.at[i, z], maps.at[i, z], (z + o) % nz, row))
+
+    def spread(layer):
+        for o in far_first(ni):
+            send(MI, o, maps.at[i, layer], maps.at[i, layer], z, rows + (i + o) % ni)
+
+    spread(z)
+    for o in far_first(nz)[::-1]:
+        source = (z + nz - o) % nz
+        await_slot(MZ, o, maps.at[i, source])
+        spread(source)
     for o in far_first(nz):
         sent.append(send(GZ, o, gain_t.at[z], gain_t.at[z], (z + o) % nz, row))
-    for o in far_first(nz)[::-1]:
-        await_slot(MZ, o, maps.at[i, (z + nz - o) % nz])
-    for o in range(1, ni):
-        sent.append(send(MI, o, maps.at[i], maps.at[i], z, rows + (i + o) % ni))
 
     for o in range(1, ni):
         await_slot(SH, o, shift_in.at[(i + ni - o) % ni])
@@ -166,26 +200,95 @@
         product = mm(jnp.concatenate(split(state), axis=0), maps[k].reshape(rank, 2 * rank))
         state = product[:tall, :rank] + (product[:tall, rank:] + product[tall:, :rank])
         state = jnp.concatenate([state[:cols] + shift_in[k], state[cols:]], axis=0)
-    total[...] = state.astype(BF16)
-
-    for d in range(ny - 1, 0, -1):
-
-        @pl.when(y + d < ny)
-        def _():
-            send(OU, d, total, total_in.at[y], z, row + d * ni)
+    half = rank // 2
+    shifts, core = pl.ds(half, cols), i % 2
+    mine = pl.ds(pl.multiple_of(core * half, half), half + cols)
+    map_mine = pl.ds(pl.multiple_of(core * (half + cols), half), half)
+    total[:half, :] = state[cols : cols + half].astype(BF16)
+    total[half : half + cols, :] = state[:cols].astype(BF16)
+    total[half + cols :, :] = state[cols + half :].astype(BF16)
+    carry[...] = inc_t[i]
+
+    def matrix_of(rows):
+        return jnp.concatenate([rows[:half], rows[half + cols :]], axis=0)
+
+    def outer_copies(act):
+        for d in far_first(ny):
+
+            @pl.when(y == 0)
+            def _():
+                act(d, total.at[shifts], total_in.at[d, shifts])
+
+            @pl.when(jnp.logical_and(y > 0, y + d < ny))
+            def _():
+                act(d, total.at[mine], total_in.at[d, mine])
+
+    @pl.when(y == 0)
+    def _():
+        product = mm(jnp.concatenate(split(carry[...]), axis=0), matrix_of(total[...]))
+        total[half : half + cols, :] = (product[:cols] + product[cols:] + state[:cols]).astype(BF16)
+
+    def outer_sent(d, source, target):
+        pltpu.make_async_remote_copy(
+            src_ref=source,
+            dst_ref=target,
+            send_sem=send_sem.at[OU, d],
+            recv_sem=recv_sem.at[OU, d],
+            device_id=(z, row + d * ni),
+            device_id_type=MESH,
+        ).wait_send()
+
+    outer_copies(lambda d, source, target: send(OU, d, source, target, z, row + d * ni))
 
     for o in far_first(nz)[::-1]:
         await_slot(GZ, o, gain_t.at[(z + nz - o) % nz])
     gain[...] = gain_t[...].reshape(rank, order).T
 
-    carry[...] = inc_t[i]
-    for k in range(ny - 1):
-
-        @pl.when(k < y)
+    def forward(d):
+        return pltpu.make_async_remote_copy(
+            src_ref=total_in.at[d, map_mine],
+            dst_ref=total_in.at[d, map_mine],
+            send_sem=send_sem.at[FW, d],
+            recv_sem=recv_sem.at[FW, d],
+            device_id=(z, row + 1 - 2 * core),
+            device_id_type=MESH,
+        )
+
+    for d in range(1, ny):
+
+        @pl.when(d < y)
         def _():
-            await_slot(OU, y - k, total_in.at[k])
-            product = mm(jnp.concatenate(split(carry[...]), axis=0), total_in[k, cols:, :])
-            carry[...] = product[:cols] + product[cols:] + total_in[k, :cols, :].astype(F32)
+            await_slot(OU, d, total_in.at[d, mine])
+            forward(d).start()
+
+        near = d - 1
+        if near < 1:
+            continue
+
+        @pl.when(near < y)
+        def _():
+            forward(near).wait_recv()
+            matrix = matrix_of(total_in[near])
+            if near == 1:
+                block[:cols, :] = total_in[near, half : half + cols, :].astype(F32)
+                block[cols:, :] = matrix.astype(F32)
+            else:
+                rows_in = jnp.concatenate([total_in[near, half : half + cols, :], matrix], axis=0)
+                product = mm(rows_in, jnp.concatenate(split(block[cols:, :]), axis=1))
+                product = product[:, :rank] + product[:, rank:]
+                block[:cols, :] += product[:cols]
+                block[cols:, :] = product[cols:]
+
+    for d in range(1, ny):
+
+        @pl.when(d == y)
+        def _():
+            await_slot(OU, d, total_in.at[d, shifts])
+            if d == 1:
+                carry[...] = total_in[d, half : half + cols, :].astype(F32)
+            else:
+                product = mm(total_in[d, half : half + cols, :], jnp.concatenate(split(block[cols:, :]), axis=1))
+                carry[...] = product[:, :rank] + product[:, rank:] + block[:cols, :]
 
     start = carry[...]
     coup[0] = start.astype(BF16)
@@ -193,7 +296,7 @@
     product = product[:cols] + product[cols:]
     for k in range(1, ni):
         coup[k] = (product[:, (k - 1) * rank : k * rank] + pre_s[k]).astype(BF16)
-    for o in range(1, ni):
+    for o in far_first(ni):
         peer = (i + o) % ni
         sent.append(send(CB, o, coup.at[peer], coup_in.at[i], z, rows + peer))
     coup_in[i] = coup[i]
@@ -207,18 +310,27 @@
 
     for copy in sent:
         copy.wait_send()
-    for d in range(1, ny):
-
-        @pl.when(y + d < ny)
+    def drain(kind, o, source):
+        pltpu.make_async_remote_copy(
+            src_ref=source,
+            dst_ref=source,
+            send_sem=send_sem.at[kind, o],
+            recv_sem=recv_sem.at[kind, o],
+            device_id=(z, row),
+            device_id_type=MESH,
+        ).wait_send()
+
+    for o in givers:
+        drain(RS, o, part.at[0])
+    for o in range(1, ni):
+        drain(MI, o, maps.at[i])
+
+    outer_copies(outer_sent)
+    for d in range(1, ny - 1):
+
+        @pl.when(d < y)
         def _():
-            pltpu.make_async_remote_copy(
-                src_ref=total,
-                dst_ref=total_in.at[y],
-                send_sem=send_sem.at[OU, d],
-                recv_sem=recv_sem.at[OU, d],
-                device_id=(z, row + d * ni),
-                device_id_type=MESH,
-            ).wait_send()
+            forward(d).wait_send()
 
 
 def solution(mesh, inner=INNER):
@@ -260,9 +372,12 @@
                 vm((cols, rank), F32),
                 vm((ni, cols, rank), BF16),
                 vm((ni, cols, rank), BF16),
+                vm((cols + rank, rank), F32),
+                vm((2, max(thick // 2, 8), order), F32),
+                vm((2, max(thick // 2, 8), order), F32),
                 pltpu.SemaphoreType.DMA((6,)),
-                pltpu.SemaphoreType.DMA((8, 8)),
-                pltpu.SemaphoreType.DMA((8, 8)),
+                pltpu.SemaphoreType.DMA((10, 8)),
+                pltpu.SemaphoreType.DMA((10, 8)),
             ],
             compiler_params=pltpu.CompilerParams(
                 collective_id=0, has_side_effects=True, vmem_limit_bytes=48 << 20

time: 56.6 us -> 50.8 us (0.90)
  the two profiles are of different devices: /device:TPU:41 before, /device:TPU:56 now
where the time goes in v3:
time: 50.8 us; the launch traced here: 49.9 us
  Pallas kernels  48.9 us (96%)
  local copies, waits for them, and re-layouts  0.97 us (2%)
    pallas_call x1, Pallas kernels, body(): pl.pallas_call(functools.partial(kernel, nz, ni, ny), out_shape=jax.Shape...  48.9 us

profile of v3, /device:TPU:56, one launch (start us, length us, event | category | flops | bytes accessed | tf_op | source)
XLA Modules:
  0.0 49.9 jit_solution(980191658377277935)
XLA Ops:
  0.0 48.9 %shard_map.73 = bf16[1024,512]{1,0:T(8,128)(2,1)S(1)} custom-call(bf16[1024,128]{1,0:T(8,128)(2,1)} %bitcast.2, bf16[1024,128]{1,0:T(8,128)(2,1)} %bitcast.3, bf16[1024,128]{1,0:T(8,128)(2,1)} %sketch.1, bf16[1024,128]{1,0:T(8,128)(2,1)} %basis.1, bf16[1024,1024]{1,0:T(8,128)(2,1)} %inverse.1, bf16[1024,512]{1,0:T(8,128)(2,1)} %rhs.1, f32[128,512]{1,0:T(8,128)} %incoming.1), custom_call_target="tpu_custom_call" | custom-call | tf_op jit(solution)/shard_map/pallas_call | solution.py:345
  48.9 1.0 %copy.9 = bf16[1024,512]{1,0:T(8,128)(2,1)} copy(bf16[1024,512]{1,0:T(8,128)(2,1)S(1)} %shard_map.73) | data formatting | bytes 2097152

commit v4 on v3

--- a/solution.py
+++ b/solution.py
@@ -26,7 +26,9 @@
     return sorted(range(1, n), key=lambda o: -min(o, n - o))
 
 
-RS, SH, MZ, GZ, MI, OU, CB, BS, FW, ME = range(10)
+RS, SH, GZ, CB, BS, ME, MZ, MI, OU, FW = range(10)
+SEND_AT = [0, 1, 2, 3, 4, 5, 6, 7, 8, 16]
+RECV_AT = [0, 1, 2, 3, 4, 5, 7, 15, 23, 31]
 
 
 def kernel(
@@ -47,6 +49,20 @@
     cols = width // ni
     thick = rank // nz
 
+    barrier = pltpu.get_barrier_semaphore()
+
+    def greet(layer, target):
+        pl.semaphore_signal(barrier, inc=1, device_id=(layer, target), device_id_type=MESH)
+
+    for o in range(1, nz):
+        greet((z + o) % nz, row)
+    for o in range(1, ni):
+        greet(z, rows + (i + o) % ni)
+    for o in range(1, ny):
+        greet(z, ((y + o) % ny) * ni + i)
+    greet(z, (row + 1) % n_row)
+    greet(z, (row + n_row - 1) % n_row)
+
     loads = [
         pltpu.make_async_copy(source, target, load_sem.at[k])
         for k, (source, target) in enumerate(
@@ -56,26 +72,16 @@
     for load in loads:
         load.start()
 
-    barrier = pltpu.get_barrier_semaphore()
-
-    def greet(layer, target):
-        pl.semaphore_signal(barrier, inc=1, device_id=(layer, target), device_id_type=MESH)
-
-    for o in range(1, nz):
-        greet((z + o) % nz, row)
-    for o in range(1, ni):
-        greet(z, rows + (i + o) % ni)
-    for o in range(1, ny):
-        greet(z, ((y + o) % ny) * ni + i)
-    greet(z, (row + 1) % n_row)
-    greet(z, (row + n_row - 1) % n_row)
+    def semaphores(kind, slot):
+        sent_at = SEND_AT[kind] + (slot if kind in (OU, FW) else 0)
+        got_at = RECV_AT[kind] + (slot if kind in (ME, MZ, MI, OU, FW) else 0)
+        return {"send_sem": send_sem.at[sent_at], "recv_sem": recv_sem.at[got_at]}
 
     def send(kind, slot, source, target, layer, dest):
         copy = pltpu.make_async_remote_copy(
             src_ref=source,
             dst_ref=target,
-            send_sem=send_sem.at[kind, slot],
-            recv_sem=recv_sem.at[kind, slot],
+            **semaphores(kind, slot),
             device_id=(layer, dest),
             device_id_type=MESH,
         )
@@ -86,13 +92,10 @@
         pltpu.make_async_remote_copy(
             src_ref=target,
             dst_ref=target,
-            send_sem=send_sem.at[kind, slot],
-            recv_sem=recv_sem.at[kind, slot],
+            **semaphores(kind, slot),
             device_id=(z, row),
             device_id_type=MESH,
         ).wait_recv()
-
-    sent = []
 
     loads[0].wait()
     loads[1].wait()
@@ -112,8 +115,8 @@
 
     if merging:
         across = (z + 4) % nz
-        sent.append(send(ME, 0, part.at[across, low], merge_in.at[0], (z + 1) % nz, row))
-        sent.append(send(ME, 1, part.at[across, high_rows], merge_in.at[1], (z + 7) % nz, row))
+        send(ME, 0, part.at[across, low], merge_in.at[0], (z + 1) % nz, row)
+        send(ME, 1, part.at[across, high_rows], merge_in.at[1], (z + 7) % nz, row)
         third, fifth = (z + 3) % nz, (z + 5) % nz
         send(RS, 3, part.at[third, high_rows], part_in.at[z, high_rows], third, row)
         send(RS, 5, part.at[fifth, low], part_in.at[z, low], fifth, row)
@@ -122,7 +125,7 @@
     else:
         for o in far_first(nz):
             give(o)
-    sent.append(send(BS, 0, basis, v_basis, z, (row + n_row - 1) % n_row))
+    send(BS, 0, basis, v_basis, z, (row + n_row - 1) % n_row)
 
     for load in loads[3:]:
         load.wait()
@@ -152,22 +155,21 @@
     shift[...] = step_shift.T.reshape(shift.shape)
     for o in range(1, ni):
         peer = (i + o) % ni
-        sent.append(send(SH, o, shift.at[peer], shift_in.at[i], z, rows + peer))
+        send(SH, o, shift.at[peer], shift_in.at[i], z, rows + peer)
     shift_in[i] = shift[i]
 
     summed = part[z]
     givers = [o for o in far_first(nz)[::-1] if not (merging and o == 4)]
+    await_slot(RS, 0, part_in.at[pl.ds(0, len(givers))])
     for o in givers:
-        source = (z + nz - o) % nz
-        await_slot(RS, o, part_in.at[source])
-        summed = summed + part_in[source]
+        summed = summed + part_in[(z + nz - o) % nz]
     range_t = (-summed).astype(BF16)
     gain_part = mm(range_t, v_invt[...]).astype(BF16)
     gain_t[z] = gain_part
     high, low = split(-mm(gain_part, v_basis[...]))
     maps[i, z] = jnp.concatenate([high, low], axis=1)
     for o in far_first(nz):
-        sent.append(send(MZ, o, maps.at[i, z], maps.at[i, z], (z + o) % nz, row))
+        send(MZ, o, maps.at[i, z], maps.at[i, z], (z + o) % nz, row)
 
     def spread(layer):
         for o in far_first(ni):
@@ -179,10 +181,9 @@
         await_slot(MZ, o, maps.at[i, source])
         spread(source)
     for o in far_first(nz):
-        sent.append(send(GZ, o, gain_t.at[z], gain_t.at[z], (z + o) % nz, row))
-
-    for o in range(1, ni):
-        await_slot(SH, o, shift_in.at[(i + ni - o) % ni])
+        send(GZ, o, gain_t.at[z], gain_t.at[z], (z + o) % nz, row)
+
+    await_slot(SH, 0, shift_in.at[pl.ds(0, ni - 1)])
 
     def arrive(k):
         @pl.when(k != i)
@@ -232,24 +233,18 @@
         pltpu.make_async_remote_copy(
             src_ref=source,
             dst_ref=target,
-            send_sem=send_sem.at[OU, d],
-            recv_sem=recv_sem.at[OU, d],
+            **semaphores(OU, d),
             device_id=(z, row + d * ni),
             device_id_type=MESH,
         ).wait_send()
 
     outer_copies(lambda d, source, target: send(OU, d, source, target, z, row + d * ni))
-
-    for o in far_first(nz)[::-1]:
-        await_slot(GZ, o, gain_t.at[(z + nz - o) % nz])
-    gain[...] = gain_t[...].reshape(rank, order).T
 
     def forward(d):
         return pltpu.make_async_remote_copy(
             src_ref=total_in.at[d, map_mine],
             dst_ref=total_in.at[d, map_mine],
-            send_sem=send_sem.at[FW, d],
-            recv_sem=recv_sem.at[FW, d],
+            **semaphores(FW, d),
             device_id=(z, row + 1 - 2 * core),
             device_id_type=MESH,
         )
@@ -298,33 +293,35 @@
         coup[k] = (product[:, (k - 1) * rank : k * rank] + pre_s[k]).astype(BF16)
     for o in far_first(ni):
         peer = (i + o) % ni
-        sent.append(send(CB, o, coup.at[peer], coup_in.at[i], z, rows + peer))
+        send(CB, o, coup.at[peer], coup_in.at[i], z, rows + peer)
     coup_in[i] = coup[i]
-    for o in range(1, ni):
-        await_slot(CB, o, coup_in.at[(i + ni - o) % ni])
+    await_slot(GZ, 0, gain_t.at[pl.ds(0, nz - 1)])
+    gain[...] = gain_t[...].reshape(rank, order).T
+    await_slot(CB, 0, coup_in.at[pl.ds(0, ni - 1)])
 
     coupled_t = coup_in[...].reshape(width, rank)
     for t in range(order // step):
         at = slice(t * step, (t + 1) * step)
         out[at, :] = (v_app[at, :].astype(F32) - mm(gain[at, :], coupled_t, 1, 1)).astype(BF16)
 
-    for copy in sent:
-        copy.wait_send()
-    def drain(kind, o, source):
+    def drain(kind, source):
         pltpu.make_async_remote_copy(
             src_ref=source,
             dst_ref=source,
-            send_sem=send_sem.at[kind, o],
-            recv_sem=recv_sem.at[kind, o],
+            **semaphores(kind, 0),
             device_id=(z, row),
             device_id_type=MESH,
         ).wait_send()
 
-    for o in givers:
-        drain(RS, o, part.at[0])
-    for o in range(1, ni):
-        drain(MI, o, maps.at[i])
-
+    drain(RS, part.at[pl.ds(0, len(givers))])
+    if merging:
+        drain(ME, merged)
+    drain(BS, v_basis)
+    drain(SH, shift.at[pl.ds(0, ni - 1)])
+    drain(MZ, maps.at[i, pl.ds(0, nz - 1)])
+    drain(MI, maps.at[pl.ds(0, ni - 1)])
+    drain(GZ, gain_t.at[pl.ds(0, nz - 1)])
+    drain(CB, coup.at[pl.ds(0, ni - 1)])
     outer_copies(outer_sent)
     for d in range(1, ny - 1):
 
@@ -376,8 +373,8 @@
                 vm((2, max(thick // 2, 8), order), F32),
                 vm((2, max(thick // 2, 8), order), F32),
                 pltpu.SemaphoreType.DMA((6,)),
-                pltpu.SemaphoreType.DMA((10, 8)),
-                pltpu.SemaphoreType.DMA((10, 8)),
+                pltpu.SemaphoreType.DMA((24,)),
+                pltpu.SemaphoreType.DMA((39,)),
             ],
             compiler_params=pltpu.CompilerParams(
                 collective_id=0, has_side_effects=True, vmem_limit_bytes=48 << 20

time: 50.8 us -> 49.7 us (0.978)
  the two profiles are of different devices: /device:TPU:56 before, /device:TPU:49 now
where the time goes in v4:
time: 49.7 us; the launch traced here: 49.6 us
  Pallas kernels  48.6 us (98%)
  local copies, waits for them, and re-layouts  0.97 us (2%)
    pallas_call x1, Pallas kernels, body(): pl.pallas_call(functools.partial(kernel, nz, ni, ny), out_shape=jax.Shape...  48.6 us

profile of v4, /device:TPU:49, one launch (start us, length us, event | category | flops | bytes accessed | tf_op | source)
XLA Modules:
  0.0 49.6 jit_solution(12474974513479213721)
XLA Ops:
  0.0 48.6 %shard_map.73 = bf16[1024,512]{1,0:T(8,128)(2,1)S(1)} custom-call(bf16[1024,128]{1,0:T(8,128)(2,1)} %bitcast.2, bf16[1024,128]{1,0:T(8,128)(2,1)} %bitcast.3, bf16[1024,128]{1,0:T(8,128)(2,1)} %sketch.1, bf16[1024,128]{1,0:T(8,128)(2,1)} %basis.1, bf16[1024,1024]{1,0:T(8,128)(2,1)} %inverse.1, bf16[1024,512]{1,0:T(8,128)(2,1)} %rhs.1, f32[128,512]{1,0:T(8,128)} %incoming.1), custom_call_target="tpu_custom_call" | custom-call | tf_op jit(solution)/shard_map/pallas_call | solution.py:342
  48.6 1.0 %copy.9 = bf16[1024,512]{1,0:T(8,128)(2,1)} copy(bf16[1024,512]{1,0:T(8,128)(2,1)S(1)} %shard_map.73) | data formatting | bytes 2097152

commit v5 on v4

--- a/solution.py
+++ b/solution.py
@@ -249,16 +249,14 @@
             device_id_type=MESH,
         )
 
-    for d in range(1, ny):
+    for d in far_first(ny):
 
         @pl.when(d < y)
         def _():
             await_slot(OU, d, total_in.at[d, mine])
             forward(d).start()
 
-        near = d - 1
-        if near < 1:
-            continue
+    for near in range(1, ny - 1):
 
         @pl.when(near < y)
         def _():

time: 49.7 us -> 48.8 us (0.982)
  the two profiles are of different devices: /device:TPU:49 before, /device:TPU:56 now
where the time goes in v5:
time: 48.8 us; the launch traced here: 48.7 us
  Pallas kernels  47.7 us (98%)
  local copies, waits for them, and re-layouts  0.97 us (2%)
    pallas_call x1, Pallas kernels, body(): pl.pallas_call(functools.partial(kernel, nz, ni, ny), out_shape=jax.Shape...  47.7 us

profile of v5, /device:TPU:56, one launch (start us, length us, event | category | flops | bytes accessed | tf_op | source)
XLA Modules:
  0.0 48.7 jit_solution(13034221787665832886)
XLA Ops:
  0.0 47.7 %shard_map.73 = bf16[1024,512]{1,0:T(8,128)(2,1)S(1)} custom-call(bf16[1024,128]{1,0:T(8,128)(2,1)} %bitcast.2, bf16[1024,128]{1,0:T(8,128)(2,1)} %bitcast.3, bf16[1024,128]{1,0:T(8,128)(2,1)} %sketch.1, bf16[1024,128]{1,0:T(8,128)(2,1)} %basis.1, bf16[1024,1024]{1,0:T(8,128)(2,1)} %inverse.1, bf16[1024,512]{1,0:T(8,128)(2,1)} %rhs.1, f32[128,512]{1,0:T(8,128)} %incoming.1), custom_call_target="tpu_custom_call" | custom-call | tf_op jit(solution)/shard_map/pallas_call | solution.py:340
  47.7 1.0 %copy.9 = bf16[1024,512]{1,0:T(8,128)(2,1)} copy(bf16[1024,512]{1,0:T(8,128)(2,1)S(1)} %shard_map.73) | data formatting | bytes 2097152
